TPU v7x, 512 devices: a whole 4x4x16 slice. The times are simulated.
512 devices in a mesh: gx: 16 (over z), gy: 32 (over y, x, core).
Axes of the slice: x: 4, y: 4, z: 16, core: 2. Of those that a mesh axis runs over, the one named last changes fastest.
Arguments:
- adjoint_guess: float32 [64, 512, 256], P('gx', 'gy'), may hold values from -80 to 80, as said below
- velocity: float32 [3, 64, 16384], P(None, 'gx', 'gy'), may hold values from -1 to 1
- leaf_rate: float32 [64, 16384], P('gx', 'gy'), may hold values from 0.2 to 5
- canopy: int32 [64, 16384], P('gx', 'gy'), may hold values from 0 to 1, as said below
- solid: int32 [64, 16384], P('gx', 'gy'), may hold values from 0 to 1, as said below
- receptors: int32 [8], replicated, may hold values from 0 to 32767
Outputs:
- adjoint_field: float32 [64, 512, 256], P('gx', 'gy')
- residual: float32 [64, 512, 256], P('gx', 'gy')
Inputs may be any that keep to these rules, and one draw needn't show every extreme that they name: `adjoint_guess`: finite values. 1 marks building cells; every horizontal column is solid from the ground up to its building's height. `canopy`: 1 marks tree-crown cells; none is solid.
All inputs are finite; a program needn't handle non-finite values.
Results may differ from a plain program's by a relative error of at most 0.0003.
Values sent between devices are 32-bit elements; how exact they have to be, the bound alone decides.
A program may use at most 64 MiB of HBM per device.

v0:
```python
import jax
import jax.numpy as jnp
from jax import lax
from jax.sharding import PartitionSpec as P

NZ = 32
R = 8
CYCLES = 3
horiz_diff = 4.0
vert_diff = 2.0
decay_rate = 3.5
penalty = 40.0
leaf_gain = 4.0
source_gain = 32.0


def padded_2(shard, sides, width):
    for axis, dim in sides:
        size, length = (lax.axis_size(axis), shard.shape[dim])
        up = [(i, (i + 1) % size) for i in range(size - 1)]
        down = [(j, i) for i, j in up]
        last = lax.slice_in_dim(shard, length - width, length, axis=dim)
        initial = lax.slice_in_dim(shard, 0, width, axis=dim)
        before = lax.ppermute(last, axis, up)
        after = lax.ppermute(initial, axis, down)
        shard = jnp.concatenate([before, shard, after], axis=dim)
    return shard


def coefficient_fields(flows, reaction):
    east_flow = flows[0]
    north_flow = flows[1]
    rise_flow = flows[2]
    couplings = [
        horiz_diff + jax.nn.relu(east_flow),
        horiz_diff + jax.nn.relu(-east_flow),
        horiz_diff + jax.nn.relu(north_flow),
        horiz_diff + jax.nn.relu(-north_flow),
        vert_diff + jax.nn.relu(rise_flow),
        vert_diff + jax.nn.relu(-rise_flow),
    ]
    diagonal = (
        decay_rate
        + reaction
        + couplings[0]
        + couplings[1]
        + couplings[2]
        + couplings[3]
        + couplings[4]
        + couplings[5]
    )
    return [jnp.repeat(piece, R, axis=-1) for piece in [diagonal] + couplings]


def apply_operator(padded, coefficients):
    centre = padded[1:-1, 1:-1]
    zero_lane = jnp.zeros(centre.shape[:-1] + (R,), jnp.float32)
    upper_cells = jnp.concatenate([centre[..., R:], zero_lane], axis=-1)
    lower_cells = jnp.concatenate([zero_lane, centre[..., :-R]], axis=-1)
    diagonal, east_c, west_c, north_c, south_c, upper_c, lower_c = coefficients
    return (
        diagonal * centre
        - east_c * padded[2:, 1:-1]
        - west_c * padded[:-2, 1:-1]
        - north_c * padded[1:-1, 2:]
        - south_c * padded[1:-1, :-2]
        - upper_c * upper_cells
        - lower_c * lower_cells
    )


def per_receptor(first, second):
    return jnp.sum((first * second).reshape(-1, R), axis=0)


def spread_lanes(values):
    return jnp.tile(values, NZ)


def residual_of(image_in, source_in):
    return source_in - image_in


def body(adjoint_guess, velocity, leaf_rate, canopy, solid, receptors):
    rows_dev = adjoint_guess.shape[0]
    cols_dev = adjoint_guess.shape[1]
    total_cols = cols_dev * lax.axis_size("gy")
    row_start = lax.axis_index("gx") * rows_dev
    col_start = lax.axis_index("gy") * cols_dev
    flows = velocity.reshape(3, rows_dev, cols_dev, NZ)
    reaction = (
        penalty * solid.astype(jnp.float32) + leaf_gain * leaf_rate * canopy.astype(jnp.float32)
    ).reshape(rows_dev, cols_dev, NZ)
    coefficients = coefficient_fields(flows, reaction)
    rec_rows = receptors // total_cols
    rec_cols = receptors % total_cols

    def operate(values):
        padded = padded_2(values, (("gx", 0), ("gy", 1)), 1)
        return apply_operator(padded, coefficients)

    global_rows = row_start + jnp.arange(rows_dev, dtype=jnp.int32)
    global_cols = col_start + jnp.arange(cols_dev, dtype=jnp.int32)
    hit_rows = (global_rows[:, None] == rec_rows[None, :]).astype(jnp.float32)
    hit_cols = (global_cols[:, None] == rec_cols[None, :]).astype(jnp.float32)
    receptor_plane = source_gain * hit_rows[:, None, :] * hit_cols[None, :, :]
    ground_lane = jnp.zeros((rows_dev, cols_dev, R), jnp.float32)
    upper_lanes = jnp.zeros((rows_dev, cols_dev, (NZ - 2) * R), jnp.float32)
    source = jnp.concatenate([ground_lane, receptor_plane, upper_lanes], axis=-1)
    iterate = adjoint_guess
    first_image = operate(iterate)
    middle = residual_of(first_image, source)
    second_image = operate(middle)
    residual = middle
    image_dir = second_image
    for cycle_index in range(CYCLES):
        if cycle_index > 0:
            image_dir = operate(residual)
        squares, against = lax.psum(
            (per_receptor(residual, residual), per_receptor(residual, image_dir)), ("gx", "gy")
        )
        alpha_step = squares / against
        halfway = residual - spread_lanes(alpha_step) * image_dir
        turned = operate(halfway)
        along_turn, turn_power = lax.psum(
            (per_receptor(turned, halfway), per_receptor(turned, turned)), ("gx", "gy")
        )
        omega_step = along_turn / turn_power
        iterate = iterate + spread_lanes(alpha_step) * residual + spread_lanes(omega_step) * halfway
        residual = halfway - spread_lanes(omega_step) * turned
    return (iterate, residual)


def solution(mesh):
    return jax.shard_map(
        body,
        mesh=mesh,
        in_specs=(
            P("gx", "gy", None),
            P(None, "gx", "gy"),
            P("gx", "gy"),
            P("gx", "gy"),
            P("gx", "gy"),
            P(),
        ),
        out_specs=(P("gx", "gy", None), P("gx", "gy", None)),
        check_vma=False,
    )
```

profile of v0, /device:TPU:1, one launch (start us, length us, event | category | flops | bytes accessed | tf_op | source)
XLA Modules:
  0.0 755.6 jit_solution(6809923909416197719)
XLA Ops:
  3.3 5.6 collective-permute-start.1
  17.2 8.3 %collective-permute-start.2 = (f32[6,1,256]{2,1,0:T(1,128)}, f32[6,1,256]{2,1,0:T(1,128)}, u32[]{:S(2)}, u32[]{:S(2)}) collective-permute-start(f32[6,1,256]{2,1,0:T(1,128)} %get-tuple-element.50), channel_id=1, source_target_pairs={{1,0},{2,1},{3,2},{4,3},{5,4},{6,5},{7,6},{8,7},{9,8},{10,9},{11,1... | collective-permute-start | bytes 18440 | tf_op jit(solution)/shard_map/ppermute | solution.py:25
  25.5 1.9 collective-permute-start.3
  34.7 3.2 collective-permute-done.4
  37.9 4.2 collective-permute-start.6
  46.1 111.9 %all-reduce.19 = (f32[8]{0:T(128)S(1)}, f32[8]{0:T(128)S(1)}) all-reduce(f32[8]{0:T(128)S(1)} %reduce_sum.108, f32[8]{0:T(128)S(1)} %reduce_sum.109), channel_id=1, replica_groups=mesh['gx'=16,'gy'=32] {'gx','gy'}, use_global_device_ids=true, to_apply=%region_1.2 | all-reduce | flops 16 | bytes 128 | tf_op jit(solution)/shard_map/psum | solution.py:119
  160.8 3.2 collective-permute-done.8
  164.0 4.1 collective-permute-start.10
  168.2 1.9 collective-permute-start.11
  173.1 104.2 %all-reduce.18 = (f32[8]{0:T(128)S(1)}, f32[8]{0:T(128)S(1)}) all-reduce(f32[8]{0:T(128)S(1)} %reduce_sum.110, f32[8]{0:T(128)S(1)} %reduce_sum.111), channel_id=1, replica_groups=mesh['gx'=16,'gy'=32] {'gx','gy'}, use_global_device_ids=true, to_apply=%region_5.6 | all-reduce | flops 16 | bytes 128 | tf_op jit(solution)/shard_map/psum | solution.py:125
  280.0 3.2 collective-permute-done.12
  283.2 3.7 collective-permute-start.14
  290.9 105.5 %all-reduce.17 = (f32[8]{0:T(128)S(1)}, f32[8]{0:T(128)S(1)}) all-reduce(f32[8]{0:T(128)S(1)} %reduce_sum.112, f32[8]{0:T(128)S(1)} %reduce_sum.113), channel_id=1, replica_groups=mesh['gx'=16,'gy'=32] {'gx','gy'}, use_global_device_ids=true, to_apply=%region_9.10 | all-reduce | flops 16 | bytes 128 | tf_op jit(solution)/shard_map/psum | solution.py:119
  399.1 3.2 collective-permute-done.16
  402.3 4.0 collective-permute-start.18
  411.3 104.9 %all-reduce.16 = (f32[8]{0:T(128)S(1)}, f32[8]{0:T(128)S(1)}) all-reduce(f32[8]{0:T(128)S(1)} %reduce_sum.114, f32[8]{0:T(128)S(1)} %reduce_sum.115), channel_id=1, replica_groups=mesh['gx'=16,'gy'=32] {'gx','gy'}, use_global_device_ids=true, to_apply=%region_13.14 | all-reduce | flops 16 | bytes 128 | tf_op jit(solution)/shard_map/psum | solution.py:125
  518.9 3.2 collective-permute-done.20
  522.1 4.0 collective-permute-start.22
  526.1 2.1 collective-permute-start.23
  530.2 104.8 %all-reduce.15 = (f32[8]{0:T(128)S(1)}, f32[8]{0:T(128)S(1)}) all-reduce(f32[8]{0:T(128)S(1)} %reduce_sum.116, f32[8]{0:T(128)S(1)} %reduce_sum.117), channel_id=1, replica_groups=mesh['gx'=16,'gy'=32] {'gx','gy'}, use_global_device_ids=true, to_apply=%region_17.18 | all-reduce | flops 16 | bytes 128 | tf_op jit(solution)/shard_map/psum | solution.py:119
  637.8 3.2 collective-permute-done.24
  640.9 4.0 collective-permute-start.26
  645.0 1.9 collective-permute-start.27
  649.9 104.9 %all-reduce.14 = (f32[8]{0:T(128)S(1)}, f32[8]{0:T(128)S(1)}) all-reduce(f32[8]{0:T(128)S(1)} %reduce_sum.118, f32[8]{0:T(128)S(1)} %reduce_sum.119), channel_id=1, replica_groups=mesh['gx'=16,'gy'=32] {'gx','gy'}, use_global_device_ids=true, to_apply=%region_21.22 | all-reduce | flops 16 | bytes 128 | tf_op jit(solution)/shard_map/psum | solution.py:125
  (191 shorter events, 53.2 us)
Async XLA Ops:
  2.0 14.5 %collective-permute-start = (f32[1,16,256]{2,1,0:T(8,128)}, f32[1,16,256]{2,1,0:T(8,128)S(1)}, u32[]{:S(2)}, u32[]{:S(2)}) collective-permute-start(f32[1,16,256]{2,1,0:T(8,128)} %get-tuple-element.78), channel_id=1, source_target_pairs={{32,0},{64,32},{96,64},{128,96},{160,128},{192,160},{224,192},{256... | collective-permute-start | bytes 49160 | tf_op jit(solution)/shard_map/ppermute | solution.py:25
  3.3 12.5 %collective-permute-start.1 = (f32[1,16,256]{2,1,0:T(8,128)}, f32[1,16,256]{2,1,0:T(8,128)}, u32[]{:S(2)}, u32[]{:S(2)}) collective-permute-start(f32[1,16,256]{2,1,0:T(8,128)} %get-tuple-element.79), channel_id=1, source_target_pairs={{0,32},{32,64},{64,96},{96,128},{128,160},{160,192},{192,224},{224... | collective-permute-start | bytes 49160 | tf_op jit(solution)/shard_map/ppermute | solution.py:24
  17.2 13.4 %collective-permute-start.2 = (f32[6,1,256]{2,1,0:T(1,128)}, f32[6,1,256]{2,1,0:T(1,128)}, u32[]{:S(2)}, u32[]{:S(2)}) collective-permute-start(f32[6,1,256]{2,1,0:T(1,128)} %get-tuple-element.50), channel_id=1, source_target_pairs={{1,0},{2,1},{3,2},{4,3},{5,4},{6,5},{7,6},{8,7},{9,8},{10,9},{11,1... | collective-permute-start | bytes 18440 | tf_op jit(solution)/shard_map/ppermute | solution.py:25
  25.5 5.1 collective-permute-start.3
  32.1 2.6 collective-permute-start.5
  33.4 4.5 collective-permute-start.4
  37.9 7.1 collective-permute-start.6
  42.1 3.1 collective-permute-start.7
  159.5 4.5 collective-permute-start.8
  164.0 6.2 collective-permute-start.10
  168.2 3.1 collective-permute-start.11
  277.4 2.6 collective-permute-start.13
  278.7 4.5 collective-permute-start.12
  283.2 6.6 collective-permute-start.14
  286.9 3.1 collective-permute-start.15
  397.8 4.5 collective-permute-start.16
  402.3 6.0 collective-permute-start.18
  406.4 3.1 collective-permute-start.19
  517.6 4.5 collective-permute-start.20
  522.1 7.1 collective-permute-start.22
  526.1 3.1 collective-permute-start.23
  636.4 4.5 collective-permute-start.24
  640.9 6.0 collective-permute-start.26
  645.0 3.1 collective-permute-start.27
  (19 other events, 33.5 us)
where the time goes:
time: 758 us; the launch traced here: 756 us
  blocking collectives  636 us (84%)
  starting transfers between devices  68.4 us (9%)
  waiting for transfers between devices  22.6 us (3%)
  local copies, waits for them, and re-layouts  19.5 us (3%)
  other arithmetic  7.63 us (1%)
    psum x3, blocking collectives, body(): lax.psum((per_receptor(residual, residual), per_receptor(residual, image_...  322 us
    psum x3, blocking collectives, body(): lax.psum((per_receptor(turned, halfway), per_receptor(turned, turned)), (...  314 us
    ppermute x14, starting transfers between devices, padded_2(): after = lax.ppermute(initial, axis, down)  41.4 us
    ppermute x14, starting transfers between devices, padded_2(): before = lax.ppermute(last, axis, up)  27 us
    ppermute x14, waiting for transfers between devices, padded_2(): after = lax.ppermute(initial, axis, down)  19.1 us
  transfers between devices with their start and end apart: 28, of which 11 were waited for; matrix products, arithmetic and copies ran while one was open for 1% of the time, Pallas kernels for 0%

commit v1 on v0

--- a/solution.py
+++ b/solution.py
@@ -12,6 +12,11 @@
 penalty = 40.0
 leaf_gain = 4.0
 source_gain = 32.0
+
+
+def by_each_axis(value, axis_one, axis_two):
+    inner = lax.psum(value, axis_one)
+    return lax.psum(inner, axis_two)
 
 
 def padded_2(shard, sides, width):
@@ -122,8 +127,8 @@
         alpha_step = squares / against
         halfway = residual - spread_lanes(alpha_step) * image_dir
         turned = operate(halfway)
-        along_turn, turn_power = lax.psum(
-            (per_receptor(turned, halfway), per_receptor(turned, turned)), ("gx", "gy")
+        along_turn, turn_power = by_each_axis(
+            (per_receptor(turned, halfway), per_receptor(turned, turned)), "gx", "gy"
         )
         omega_step = along_turn / turn_power
         iterate = iterate + spread_lanes(alpha_step) * residual + spread_lanes(omega_step) * halfway

time: 758 us -> 720 us (0.950)
  blocking collectives: 636 us -> 599 us
    psum x3 -> x6, blocking collectives: 314 us -> 279 us  [the longest x3 208 us: by_each_axis(): return lax.psum(inner, axis_two)]
  transfers between devices with their start and end apart: 28 -> 28, of which waited for: 11 -> 12; matrix products, arithmetic and copies ran while one was open for 1% -> 2% of each run, Pallas kernels for 0% -> 0%
where the time goes in v1:
time: 720 us; the launch traced here: 718 us
  blocking collectives  599 us (83%)
  starting transfers between devices  67.7 us (9%)
  waiting for transfers between devices  22.7 us (3%)
  local copies, waits for them, and re-layouts  19.5 us (3%)
  other arithmetic  7.57 us (1%)
    psum x3, blocking collectives, body(): lax.psum((per_receptor(residual, residual), per_receptor(residual, image_...  320 us
    psum x3, blocking collectives, by_each_axis(): return lax.psum(inner, axis_two)  208 us
    psum x3, blocking collectives, by_each_axis(): inner = lax.psum(value, axis_one)  70.8 us
    ppermute x14, starting transfers between devices, padded_2(): after = lax.ppermute(initial, axis, down)  40.9 us
    ppermute x14, starting transfers between devices, padded_2(): before = lax.ppermute(last, axis, up)  26.8 us
    ppermute x14, waiting for transfers between devices, padded_2(): after = lax.ppermute(initial, axis, down)  19.1 us
  transfers between devices with their start and end apart: 28, of which 12 were waited for; matrix products, arithmetic and copies ran while one was open for 2% of the time, Pallas kernels for 0%

profile of v1, /device:TPU:1, one launch (start us, length us, event | category | flops | bytes accessed | tf_op | source)
XLA Modules:
  0.0 717.8 jit_solution(13875462248347872372)
XLA Ops:
  3.3 5.6 collective-permute-start.1
  17.1 8.3 %collective-permute-start.2 = (f32[6,1,256]{2,1,0:T(1,128)}, f32[6,1,256]{2,1,0:T(1,128)}, u32[]{:S(2)}, u32[]{:S(2)}) collective-permute-start(f32[6,1,256]{2,1,0:T(1,128)} %get-tuple-element.56), channel_id=1, source_target_pairs={{1,0},{2,1},{3,2},{4,3},{5,4},{6,5},{7,6},{8,7},{9,8},{10,9},{11,1... | collective-permute-start | bytes 18440 | tf_op jit(solution)/shard_map/ppermute | solution.py:30
  25.4 1.9 collective-permute-start.3
  34.7 3.2 collective-permute-done.4
  37.8 4.2 collective-permute-start.6
  46.1 111.9 %all-reduce.16 = (f32[8]{0:T(128)S(1)}, f32[8]{0:T(128)S(1)}) all-reduce(f32[8]{0:T(128)S(1)} %reduce_sum.108, f32[8]{0:T(128)S(1)} %reduce_sum.109), channel_id=1, replica_groups=mesh['gx'=16,'gy'=32] {'gx','gy'}, use_global_device_ids=true, to_apply=%region_1.2 | all-reduce | flops 16 | bytes 128 | tf_op jit(solution)/shard_map/psum | solution.py:124
  160.7 3.2 collective-permute-done.8
  163.9 4.1 collective-permute-start.10
  173.0 23.5 %all-reduce.22 = (f32[8]{0:T(128)S(1)}, f32[8]{0:T(128)S(1)}) all-reduce(f32[8]{0:T(128)S(1)} %reduce_sum.110, f32[8]{0:T(128)S(1)} %reduce_sum.111), channel_id=1, replica_groups=mesh['gx'=16,'gy'=32] {'gx'}, use_global_device_ids=true, to_apply=%region_5.6 | all-reduce | flops 16 | bytes 128 | tf_op jit(solution)/shard_map/psum | solution.py:18
  196.5 69.4 %all-reduce.19 = (f32[8]{0:T(128)S(1)}, f32[8]{0:T(128)S(1)}) all-reduce(f32[8]{0:T(128)S(1)} %get-tuple-element.24, f32[8]{0:T(128)S(1)} %get-tuple-element.25), channel_id=1, replica_groups=mesh['gx'=16,'gy'=32] {'gy'}, use_global_device_ids=true, to_apply=%region_6.7 | all-reduce | flops 16 | bytes 128 | tf_op jit(solution)/shard_map/psum | solution.py:19
  268.7 3.2 collective-permute-done.12
  271.9 3.7 collective-permute-start.14
  279.6 103.9 %all-reduce.15 = (f32[8]{0:T(128)S(1)}, f32[8]{0:T(128)S(1)}) all-reduce(f32[8]{0:T(128)S(1)} %reduce_sum.112, f32[8]{0:T(128)S(1)} %reduce_sum.113), channel_id=1, replica_groups=mesh['gx'=16,'gy'=32] {'gx','gy'}, use_global_device_ids=true, to_apply=%region_11.12 | all-reduce | flops 16 | bytes 128 | tf_op jit(solution)/shard_map/psum | solution.py:124
  386.3 3.2 collective-permute-done.16
  389.5 3.9 collective-permute-start.18
  398.3 23.6 %all-reduce.21 = (f32[8]{0:T(128)S(1)}, f32[8]{0:T(128)S(1)}) all-reduce(f32[8]{0:T(128)S(1)} %reduce_sum.114, f32[8]{0:T(128)S(1)} %reduce_sum.115), channel_id=1, replica_groups=mesh['gx'=16,'gy'=32] {'gx'}, use_global_device_ids=true, to_apply=%region_15.16 | all-reduce | flops 16 | bytes 128 | tf_op jit(solution)/shard_map/psum | solution.py:18
  422.0 69.4 %all-reduce.18 = (f32[8]{0:T(128)S(1)}, f32[8]{0:T(128)S(1)}) all-reduce(f32[8]{0:T(128)S(1)} %get-tuple-element.22, f32[8]{0:T(128)S(1)} %get-tuple-element.23), channel_id=1, replica_groups=mesh['gx'=16,'gy'=32] {'gy'}, use_global_device_ids=true, to_apply=%region_16.17 | all-reduce | flops 16 | bytes 128 | tf_op jit(solution)/shard_map/psum | solution.py:19
  494.1 3.2 collective-permute-done.20
  497.3 3.7 collective-permute-start.22
  505.1 104.1 %all-reduce.14 = (f32[8]{0:T(128)S(1)}, f32[8]{0:T(128)S(1)}) all-reduce(f32[8]{0:T(128)S(1)} %reduce_sum.116, f32[8]{0:T(128)S(1)} %reduce_sum.117), channel_id=1, replica_groups=mesh['gx'=16,'gy'=32] {'gx','gy'}, use_global_device_ids=true, to_apply=%region_21.22 | all-reduce | flops 16 | bytes 128 | tf_op jit(solution)/shard_map/psum | solution.py:124
  611.9 3.2 collective-permute-done.24
  615.1 3.9 collective-permute-start.26
  624.0 23.6 %all-reduce.20 = (f32[8]{0:T(128)S(1)}, f32[8]{0:T(128)S(1)}) all-reduce(f32[8]{0:T(128)S(1)} %reduce_sum.118, f32[8]{0:T(128)S(1)} %reduce_sum.119), channel_id=1, replica_groups=mesh['gx'=16,'gy'=32] {'gx'}, use_global_device_ids=true, to_apply=%region_25.26 | all-reduce | flops 16 | bytes 128 | tf_op jit(solution)/shard_map/psum | solution.py:18
  647.6 69.4 %all-reduce.17 = (f32[8]{0:T(128)S(1)}, f32[8]{0:T(128)S(1)}) all-reduce(f32[8]{0:T(128)S(1)} %get-tuple-element.20, f32[8]{0:T(128)S(1)} %get-tuple-element.21), channel_id=1, replica_groups=mesh['gx'=16,'gy'=32] {'gy'}, use_global_device_ids=true, to_apply=%region_26.27 | all-reduce | flops 16 | bytes 128 | tf_op jit(solution)/shard_map/psum | solution.py:19
  (194 shorter events, 59.1 us)
Async XLA Ops:
  2.0 14.5 %collective-permute-start = (f32[1,16,256]{2,1,0:T(8,128)}, f32[1,16,256]{2,1,0:T(8,128)S(1)}, u32[]{:S(2)}, u32[]{:S(2)}) collective-permute-start(f32[1,16,256]{2,1,0:T(8,128)} %get-tuple-element.84), channel_id=1, source_target_pairs={{32,0},{64,32},{96,64},{128,96},{160,128},{192,160},{224,192},{256... | collective-permute-start | bytes 49160 | tf_op jit(solution)/shard_map/ppermute | solution.py:30
  3.3 12.4 %collective-permute-start.1 = (f32[1,16,256]{2,1,0:T(8,128)}, f32[1,16,256]{2,1,0:T(8,128)}, u32[]{:S(2)}, u32[]{:S(2)}) collective-permute-start(f32[1,16,256]{2,1,0:T(8,128)} %get-tuple-element.85), channel_id=1, source_target_pairs={{0,32},{32,64},{64,96},{96,128},{128,160},{160,192},{192,224},{224... | collective-permute-start | bytes 49160 | tf_op jit(solution)/shard_map/ppermute | solution.py:29
  17.1 13.4 %collective-permute-start.2 = (f32[6,1,256]{2,1,0:T(1,128)}, f32[6,1,256]{2,1,0:T(1,128)}, u32[]{:S(2)}, u32[]{:S(2)}) collective-permute-start(f32[6,1,256]{2,1,0:T(1,128)} %get-tuple-element.56), channel_id=1, source_target_pairs={{1,0},{2,1},{3,2},{4,3},{5,4},{6,5},{7,6},{8,7},{9,8},{10,9},{11,1... | collective-permute-start | bytes 18440 | tf_op jit(solution)/shard_map/ppermute | solution.py:30
  25.4 5.1 collective-permute-start.3
  33.4 4.5 collective-permute-start.4
  37.8 7.1 collective-permute-start.6
  42.0 3.1 collective-permute-start.7
  158.1 2.6 collective-permute-start.9
  159.4 4.5 collective-permute-start.8
  163.9 6.2 collective-permute-start.10
  168.1 3.1 collective-permute-start.11
  266.1 2.6 collective-permute-start.13
  267.4 4.5 collective-permute-start.12
  271.9 6.6 collective-permute-start.14
  275.6 3.1 collective-permute-start.15
  385.0 4.5 collective-permute-start.16
  389.5 5.9 collective-permute-start.18
  393.4 3.1 collective-permute-start.19
  492.8 4.5 collective-permute-start.20
  497.3 6.6 collective-permute-start.22
  501.0 3.1 collective-permute-start.23
  610.6 4.5 collective-permute-start.24
  615.1 5.9 collective-permute-start.26
  619.0 3.1 collective-permute-start.27
  (19 other events, 33.1 us)
